TPU v7x, 256 devices: a whole 4x4x8 slice. The times are simulated.
256 devices in a mesh: layer: 8 (over x_lo, y), dp: 32 (over z, x_hi, core).
Axes of the slice: x: 4 (x_hi: 2, x_lo: 2; x = x_hi * 2 + x_lo), y: 4, z: 8, core: 2. Of those that a mesh axis runs over, the one named last changes fastest.
Arguments:
- states: bfloat16 [16, 64, 32, 32, 256], P('layer', 'dp'), may hold values from -6 to 6
- slopes: bfloat16 [16, 64, 32, 32, 256], P('layer', 'dp'), may hold values from 0.099609375 to 1
- kernels: bfloat16 [16, 9, 256, 256], P('layer'), may hold values from -0.125 to 0.125
- guess: float32 [16, 64, 32, 32, 256], P('layer', 'dp'), may hold values from -6 to 6
Outputs:
- lower_adjoint: float32 [8, 64, 32, 32, 256], P('layer', 'dp')
- kernel_grad: float32 [16, 9, 256, 256], P('layer', None, 'dp')
All inputs are finite; a program needn't handle non-finite values.
Results may differ from a plain program's by a relative error of at most 0.005.
Values sent between devices are 32-bit elements; how exact they have to be, the bound alone decides.
A program may use at most 64 MiB of HBM per device.

v0:
```python
import jax
import jax.numpy as jnp
from jax import lax
from jax.sharding import PartitionSpec as P

step_size = 0.5


def from_behind(array, axis, by):
    devices = lax.axis_size(axis)
    pairs = [(i, i + by) for i in range(devices) if 0 <= i + by < devices]
    return lax.ppermute(array, axis, pairs)


def forward_patches(images):
    image_height = images.shape[1]
    image_width = images.shape[2]
    padded = jnp.pad(images, ((0, 0), (1, 1), (1, 1), (0, 0)))
    pieces = [
        padded[:, row_shift : row_shift + image_height, col_shift : col_shift + image_width, :]
        for row_shift in range(3)
        for col_shift in range(3)
    ]
    return jnp.stack(pieces, axis=3)


def backward_patches(images):
    image_height = images.shape[1]
    image_width = images.shape[2]
    padded = jnp.pad(images, ((0, 0), (1, 1), (1, 1), (0, 0)))
    pieces = [
        padded[
            :,
            2 - row_shift : 2 - row_shift + image_height,
            2 - col_shift : 2 - col_shift + image_width,
            :,
        ]
        for row_shift in range(3)
        for col_shift in range(3)
    ]
    return jnp.stack(pieces, axis=3)


def transpose_conv(cotangent, kernel):
    pieces = backward_patches(cotangent)
    return jnp.einsum("iyxtc,tdc->iyxd", pieces, kernel, preferred_element_type=jnp.float32)


def correlate(inputs, cotangent):
    pieces = forward_patches(inputs)
    return jnp.einsum("iyxtd,iyxc->tdc", pieces, cotangent, preferred_element_type=jnp.float32)


def apply_layer(adjoint, slope, kernel, factor):
    cotangent = (slope.astype(jnp.float32) * adjoint).astype(jnp.bfloat16)
    return (adjoint + factor * transpose_conv(cotangent, kernel), cotangent)


def on_device(states, slopes, kernels, guess):
    layer_count = states.shape[0]
    image_count = states.shape[1]
    sections = lax.axis_size("layer")
    position = lax.axis_index("layer")
    replicas = lax.axis_size("dp")
    section_end, unused = apply_layer(guess[0], slopes[0], kernels[0], step_size)
    guess_last = guess[layer_count - 1]
    coarse_factor = step_size * layer_count

    def advance(current):
        return apply_layer(current, slopes[0], kernels[0], coarse_factor)[0] + section_end

    def resting(current):
        return jnp.zeros_like(current)

    def advance_turn(moment, corrections):
        sending = lax.cond(position == sections - 1 - moment, advance, resting, corrections)
        arrived_top = from_behind(sending, "layer", -1)
        return jnp.where(position == sections - 2 - moment, arrived_top - guess_last, corrections)

    starting = jnp.zeros_like(guess_last)
    corrections = lax.fori_loop(0, sections - 1, advance_turn, starting)
    adjoint = guess_last + corrections
    grad_scale = step_size / (image_count * replicas)
    gradients = [None] * layer_count
    for inner_layer in range(layer_count - 1, -1, -1):
        adjoint, cotangent = apply_layer(
            adjoint, slopes[inner_layer], kernels[inner_layer], step_size
        )
        local_term = correlate(states[inner_layer], cotangent) * grad_scale
        gradients[inner_layer] = local_term
    summed = lax.psum_scatter(jnp.stack(gradients), "dp", scatter_dimension=2, tiled=True)
    return (adjoint[None], summed)


def solution(mesh):
    return jax.shard_map(
        on_device,
        mesh=mesh,
        in_specs=(
            P("layer", "dp", None, None, None),
            P("layer", "dp", None, None, None),
            P("layer", None, None, None),
            P("layer", "dp", None, None, None),
        ),
        out_specs=(P("layer", "dp", None, None, None), P("layer", None, "dp", None)),
        check_vma=False,
    )
```

profile of v0, /device:TPU:1, one launch (start us, length us, event | category | flops | bytes accessed | tf_op | source)
XLA Modules:
  0.0 618.7 jit_solution(8489711255886549974)
XLA Ops:
  7.2 3.3 slice_bitcast_fusion
  10.6 2.2 fusion.28
  15.8 0.5 fusion.55
  16.3 4.2 fusion.35
  20.5 431.3 %while.14 = (s32[]{:T(128)}, f32[2,32,32,256]{3,2,1,0:T(8,128)S(1)}, s32[]{:T(128)}, bf16[2,2,32,32,256]{4,3,2,1,0:T(8,128)(2,1)}, bf16[2,9,256,256]{3,2,1,0:T(8...) while((s32[]{:T(128)}, ...), condition=%wide.region_3.4_spmd.clone, body=%wide.region_0.3_spmd.clone.sunk | while | flops 2420637696 | bytes 87163208 | solution.py:81
  21.0 1.6 broadcast_select_fusion.2
  22.6 1.6 conditional.3
  22.6 1.6 broadcast.8
  24.2 1.3 collective-permute-start
  25.5 46.1 %collective-permute-done = f32[2,32,32,256]{3,2,1,0:T(8,128)} collective-permute-done((f32[2,32,32,256]{3,2,1,0:T(8,128)}, f32[2,32,32,256]{3,2,1,0:T(8,128)}, u32[]{:S(2)}, u32[]{:S(2)}) %collective-permute-start) | collective-permute-done | bytes 2097184 | tf_op jit(solution)/shard_map/while/body/eval_jaxpr/ppermute | solution.py:12
  71.7 3.3 subtract_select_fusion.2
  75.0 1.6 broadcast_select_fusion.2
  76.6 1.6 conditional.3
  76.6 1.6 broadcast.8
  78.2 1.3 collective-permute-start
  79.5 48.4 %collective-permute-done = f32[2,32,32,256]{3,2,1,0:T(8,128)} collective-permute-done((f32[2,32,32,256]{3,2,1,0:T(8,128)}, f32[2,32,32,256]{3,2,1,0:T(8,128)}, u32[]{:S(2)}, u32[]{:S(2)}) %collective-permute-start) | collective-permute-done | bytes 2097184 | tf_op jit(solution)/shard_map/while/body/eval_jaxpr/ppermute | solution.py:12
  127.9 3.3 subtract_select_fusion.2
  131.2 1.6 broadcast_select_fusion.2
  132.8 1.6 conditional.3
  132.8 1.6 broadcast.8
  134.4 1.3 collective-permute-start
  135.7 45.6 %collective-permute-done = f32[2,32,32,256]{3,2,1,0:T(8,128)} collective-permute-done((f32[2,32,32,256]{3,2,1,0:T(8,128)}, f32[2,32,32,256]{3,2,1,0:T(8,128)}, u32[]{:S(2)}, u32[]{:S(2)}) %collective-permute-start) | collective-permute-done | bytes 2097184 | tf_op jit(solution)/shard_map/while/body/eval_jaxpr/ppermute | solution.py:12
  181.3 3.3 subtract_select_fusion.2
  184.6 1.6 broadcast_select_fusion.2
  186.2 1.6 conditional.3
  186.2 1.6 broadcast.8
  187.8 1.3 collective-permute-start
  189.1 47.8 %collective-permute-done = f32[2,32,32,256]{3,2,1,0:T(8,128)} collective-permute-done((f32[2,32,32,256]{3,2,1,0:T(8,128)}, f32[2,32,32,256]{3,2,1,0:T(8,128)}, u32[]{:S(2)}, u32[]{:S(2)}) %collective-permute-start) | collective-permute-done | bytes 2097184 | tf_op jit(solution)/shard_map/while/body/eval_jaxpr/ppermute | solution.py:12
  236.9 3.3 subtract_select_fusion.2
  240.3 1.6 broadcast_select_fusion.2
  241.9 1.6 conditional.3
  241.9 1.6 broadcast.8
  243.5 1.3 collective-permute-start
  244.8 45.8 %collective-permute-done = f32[2,32,32,256]{3,2,1,0:T(8,128)} collective-permute-done((f32[2,32,32,256]{3,2,1,0:T(8,128)}, f32[2,32,32,256]{3,2,1,0:T(8,128)}, u32[]{:S(2)}, u32[]{:S(2)}) %collective-permute-start) | collective-permute-done | bytes 2097184 | tf_op jit(solution)/shard_map/while/body/eval_jaxpr/ppermute | solution.py:12
  290.6 3.3 subtract_select_fusion.2
  293.9 1.6 broadcast_select_fusion.2
  295.5 1.6 conditional.3
  295.5 1.6 broadcast.8
  297.1 1.3 collective-permute-start
  298.4 44.9 %collective-permute-done = f32[2,32,32,256]{3,2,1,0:T(8,128)} collective-permute-done((f32[2,32,32,256]{3,2,1,0:T(8,128)}, f32[2,32,32,256]{3,2,1,0:T(8,128)}, u32[]{:S(2)}, u32[]{:S(2)}) %collective-permute-start) | collective-permute-done | bytes 2097184 | tf_op jit(solution)/shard_map/while/body/eval_jaxpr/ppermute | solution.py:12
  343.3 3.3 subtract_select_fusion.2
  346.7 1.6 broadcast_select_fusion.2
  348.3 1.6 conditional.3
  348.3 1.6 broadcast.8
  349.9 1.3 collective-permute-start
  351.2 97.1 %collective-permute-done = f32[2,32,32,256]{3,2,1,0:T(8,128)} collective-permute-done((f32[2,32,32,256]{3,2,1,0:T(8,128)}, f32[2,32,32,256]{3,2,1,0:T(8,128)}, u32[]{:S(2)}, u32[]{:S(2)}) %collective-permute-start) | collective-permute-done | bytes 2097184 | tf_op jit(solution)/shard_map/while/body/eval_jaxpr/ppermute | solution.py:12
  448.3 3.3 subtract_select_fusion.2
  451.8 2.5 fusion.31
  454.8 0.5 fusion.61
  456.4 0.5 fusion.67
  457.5 2.8 fusion.22
  460.4 0.9 fusion.29
  461.5 0.6 copy.74
  463.6 0.6 copy.75
  465.6 1.4 bitcast_dynamic-update-slice_fusion.1
  467.1 0.5 fusion.115
  468.8 0.5 fusion.99
  470.3 3.1 fusion.26
  473.4 3.2 fusion.27
  476.6 2.5 pad_maximum_fusion
  481.2 0.8 fusion.83
  482.6 2.8 fusion.20
  485.4 2.3 fusion.33
  487.7 123.8 %reduce-scatter.2.cloned.1.call-done = f32[2,9,8,256]{3,2,1,0:T(8,128)} async-done(((f32[2,9,256,256]{3,2,1,0:T(8,128)}), f32[2,9,8,256]{3,2,1,0:T(8,128)}) %reduce-scatter.2.cloned.1.call-update) | async-done | bytes 147472 | tf_op jit(solution)/shard_map/reduce_scatter | solution.py:91
  (63 shorter events, 13.0 us)
Async XLA Ops:
  7.2 604.4 %reduce-scatter.2.cloned.1.call-start = ((), (), s32[]{:S(2)}) async-start(), calls=%async_computation.1 | async-start | bytes 4866048 | tf_op jit(solution)/shard_map/reduce_scatter | solution.py:91
  7.2 7.1 %copy-start.1 = (bf16[2,2,32,32,256]{4,3,2,1,0:T(8,128)(2,1)S(1)}, bf16[2,2,32,32,256]{4,3,2,1,0:T(8,128)(2,1)}, u32[]{:S(2)}) copy-start(bf16[2,2,32,32,256]{4,3,2,1,0:T(8,128)(2,1)} %param.9) | copy-start | bytes 6291460
  7.2 7.1 %copy-start.3 = (f32[2,2,32,32,256]{4,3,2,1,0:T(8,128)S(1)}, f32[2,2,32,32,256]{4,3,2,1,0:T(8,128)}, u32[]{:S(2)}) copy-start(f32[2,2,32,32,256]{4,3,2,1,0:T(8,128)} %param.11) | copy-start | bytes 12582916
  13.2 3.2 copy-start.9
  24.2 47.4 %collective-permute-start = (f32[2,32,32,256]{3,2,1,0:T(8,128)}, f32[2,32,32,256]{3,2,1,0:T(8,128)}, u32[]{:S(2)}, u32[]{:S(2)}) collective-permute-start(f32[2,32,32,256]{3,2,1,0:T(8,128)} %get-tuple-element.264), channel_id=1, source_target_pairs={{32,0},{64,32},{96,64},{128,96},{160,128},{192,160},{224,192},{33,... | collective-permute-start | bytes 6291464 | tf_op jit(solution)/shard_map/while/body/eval_jaxpr/ppermute | solution.py:12
  78.2 49.7 %collective-permute-start = (f32[2,32,32,256]{3,2,1,0:T(8,128)}, f32[2,32,32,256]{3,2,1,0:T(8,128)}, u32[]{:S(2)}, u32[]{:S(2)}) collective-permute-start(f32[2,32,32,256]{3,2,1,0:T(8,128)} %get-tuple-element.264), channel_id=1, source_target_pairs={{32,0},{64,32},{96,64},{128,96},{160,128},{192,160},{224,192},{33,... | collective-permute-start | bytes 6291464 | tf_op jit(solution)/shard_map/while/body/eval_jaxpr/ppermute | solution.py:12
  134.4 46.8 %collective-permute-start = (f32[2,32,32,256]{3,2,1,0:T(8,128)}, f32[2,32,32,256]{3,2,1,0:T(8,128)}, u32[]{:S(2)}, u32[]{:S(2)}) collective-permute-start(f32[2,32,32,256]{3,2,1,0:T(8,128)} %get-tuple-element.264), channel_id=1, source_target_pairs={{32,0},{64,32},{96,64},{128,96},{160,128},{192,160},{224,192},{33,... | collective-permute-start | bytes 6291464 | tf_op jit(solution)/shard_map/while/body/eval_jaxpr/ppermute | solution.py:12
  187.8 49.1 %collective-permute-start = (f32[2,32,32,256]{3,2,1,0:T(8,128)}, f32[2,32,32,256]{3,2,1,0:T(8,128)}, u32[]{:S(2)}, u32[]{:S(2)}) collective-permute-start(f32[2,32,32,256]{3,2,1,0:T(8,128)} %get-tuple-element.264), channel_id=1, source_target_pairs={{32,0},{64,32},{96,64},{128,96},{160,128},{192,160},{224,192},{33,... | collective-permute-start | bytes 6291464 | tf_op jit(solution)/shard_map/while/body/eval_jaxpr/ppermute | solution.py:12
  243.5 47.1 %collective-permute-start = (f32[2,32,32,256]{3,2,1,0:T(8,128)}, f32[2,32,32,256]{3,2,1,0:T(8,128)}, u32[]{:S(2)}, u32[]{:S(2)}) collective-permute-start(f32[2,32,32,256]{3,2,1,0:T(8,128)} %get-tuple-element.264), channel_id=1, source_target_pairs={{32,0},{64,32},{96,64},{128,96},{160,128},{192,160},{224,192},{33,... | collective-permute-start | bytes 6291464 | tf_op jit(solution)/shard_map/while/body/eval_jaxpr/ppermute | solution.py:12
  297.1 46.2 %collective-permute-start = (f32[2,32,32,256]{3,2,1,0:T(8,128)}, f32[2,32,32,256]{3,2,1,0:T(8,128)}, u32[]{:S(2)}, u32[]{:S(2)}) collective-permute-start(f32[2,32,32,256]{3,2,1,0:T(8,128)} %get-tuple-element.264), channel_id=1, source_target_pairs={{32,0},{64,32},{96,64},{128,96},{160,128},{192,160},{224,192},{33,... | collective-permute-start | bytes 6291464 | tf_op jit(solution)/shard_map/while/body/eval_jaxpr/ppermute | solution.py:12
  349.9 98.4 %collective-permute-start = (f32[2,32,32,256]{3,2,1,0:T(8,128)}, f32[2,32,32,256]{3,2,1,0:T(8,128)}, u32[]{:S(2)}, u32[]{:S(2)}) collective-permute-start(f32[2,32,32,256]{3,2,1,0:T(8,128)} %get-tuple-element.264), channel_id=1, source_target_pairs={{32,0},{64,32},{96,64},{128,96},{160,128},{192,160},{224,192},{33,... | collective-permute-start | bytes 6291464 | tf_op jit(solution)/shard_map/while/body/eval_jaxpr/ppermute | solution.py:12
  454.3 3.2 copy-start.11
  457.5 2.8 copy-start.2
  457.5 2.8 copy-start.4
  457.5 3.8 copy-start.8
  460.3 2.6 copy-start.6
  479.2 3.3 copy-start.12
  482.5 2.8 copy-start.5
  482.5 2.9 copy-start.7
Sparse Core Ops, SparseCore 0:
  479.3 132.2 reduce-scatter.1
where the time goes:
time: 627 us; the launch traced here: 619 us
  waiting for transfers between devices  500 us (80%)
  other arithmetic  45.3 us (7%)
  local copies, waits for them, and re-layouts  33 us (5%)
  matrix products  16 us (3%)
  between operations  14.8 us (2%)
  starting transfers between devices  9 us (1%)
    ppermute x7, waiting for transfers between devices, from_behind(): return lax.ppermute(array, axis, pairs)  376 us
    reduce_scatter x1, waiting for transfers between devices, on_device(): lax.psum_scatter(jnp.stack(gradients), 'dp', scatter_dimension=2, tiled=T...  124 us
    select_n x7, other arithmetic, advance_turn(): jnp.where(position == sections - 2 - moment, arrived_top - guess_last, co...  23.1 us
    unnamed x62, local copies, waits for them, and re-layouts  15.7 us
  transfers between devices with their start and end apart: 8, of which 8 were waited for; matrix products, arithmetic and copies ran while one was open for 1% of the time, Pallas kernels for 0%

commit v1 on v0

v1 whole, which is shorter than its diff:
```python
import functools

import jax
import jax.numpy as jnp
from jax import lax
from jax.experimental import pallas as pl
from jax.experimental.pallas import tpu as pltpu
from jax.sharding import PartitionSpec as P

MESH = pl.DeviceIdType.MESH
STEP = 0.5
TOP = 8
ROWS = 88
R = 2
Q = 4
BLK = R * Q


def chain_kernel(
    sections, scale, height, width, chans,
    states_hbm, slopes_hbm, kernels_hbm, guess_hbm,
    lower_hbm, grad_hbm,
    states, slopes, kern, last, ends, recv, send, mid, low, z_chain, z_up, z_dn, grad,
    load_sems, send_sems, recv_sems, out_sems,
):
    s = lax.axis_index("layer")
    h = sections - 1 - s
    pix = height * width
    image_row = (1, height + 2)
    end_row = 2 * height + 1

    def rows(start, count):
        return pl.ds(pl.multiple_of((start + TOP) * width, width), count * width)

    def image(ref, i):
        return ref.at[rows(image_row[i], height)]

    def load(src, dst, sem):
        copy = pltpu.make_async_copy(src, dst, sem)
        copy.start()
        return copy

    pads = ((-TOP, TOP + 1), (height + 1, 1), (end_row + 1, ROWS - TOP - end_row - 1))

    def clear(ref):
        for start, count in pads:
            part = ref.at[rows(start, count)]
            part[...] = jnp.zeros(part.shape, part.dtype)

    first = [load(kernels_hbm.at[0], kern.at[0], load_sems.at[0])]
    for i in range(2):
        first.append(load(guess_hbm.at[0, i], image(ends, i), load_sems.at[1 + i]))
        first.append(load(slopes_hbm.at[0, i], image(slopes.at[0], i), load_sems.at[3 + i]))
    rest = [load(kernels_hbm.at[1], kern.at[1], load_sems.at[5])]
    for i in range(2):
        rest.append(load(guess_hbm.at[1, i], image(last, i), load_sems.at[6 + i]))
        rest.append(load(slopes_hbm.at[1, i], image(slopes.at[1], i), load_sems.at[8 + i]))
        for l in range(2):
            rest.append(load(states_hbm.at[l, i], image(states.at[l], i), load_sems.at[10 + 2 * l + i]))

    clear(recv)
    barrier = pltpu.get_barrier_semaphore()

    @pl.when(s > 0)
    def _():
        pl.semaphore_signal(barrier, inc=1, device_id={"layer": s - 1}, device_id_type=MESH)

    @pl.when(s < sections - 1)
    def _():
        pl.semaphore_signal(barrier, inc=1, device_id={"layer": s + 1}, device_id_type=MESH)

    clear(ends)
    clear(last)
    clear(slopes.at[0])
    clear(slopes.at[1])
    clear(states.at[0])
    clear(states.at[1])
    for ref in (z_chain, z_up, z_dn):
        clear(ref)
    z_up[rows(-TOP, TOP + 4)] = jnp.zeros(((TOP + 4) * width, 3 * chans), jnp.bfloat16)
    z_dn[rows(-TOP, TOP + 4)] = jnp.zeros(((TOP + 4) * width, 3 * chans), jnp.bfloat16)
    grad[...] = jnp.zeros(grad.shape, jnp.float32)

    for copy in first:
        copy.wait()

    def spread(z, start, count, slope, values):
        cot = slope.astype(jnp.float32) * values
        size = count * width
        col = lax.broadcasted_iota(jnp.int32, (size, chans), 0) % width
        z[rows(start, count), chans:2 * chans] = cot.astype(jnp.bfloat16)
        ahead = jnp.where(col == width - 1, 0.0, pltpu.roll(cot, size - 1, 0))
        z[rows(start, count), 0:chans] = ahead.astype(jnp.bfloat16)
        behind = jnp.where(col == 0, 0.0, pltpu.roll(cot, 1, 0))
        z[rows(start, count), 2 * chans:3 * chans] = behind.astype(jnp.bfloat16)

    def conv(z, layer, start, count):
        total = None
        for a in range(3):
            for b in range(3):
                piece = z[rows(start + 1 - a, count), b * chans:(b + 1) * chans]
                term = lax.dot_general(
                    piece, kern[layer, 3 * a + b], (((1,), (1,)), ((), ())),
                    preferred_element_type=jnp.float32,
                )
                total = term if total is None else total + term
        return total

    def sends(k, hop):
        start = R * k + 1 - hop
        return (start + R - 1 >= 1) & (start <= end_row)

    def chunk(src, k):
        where = rows(R * k + 1 - h, R)
        return pltpu.make_async_remote_copy(
            src_ref=src.at[where],
            dst_ref=recv.at[where],
            send_sem=send_sems.at[k],
            recv_sem=recv_sems.at[k],
            device_id={"layer": s - 1},
            device_id_type=MESH,
        )

    def arrival(k):
        where = rows(R * k + 2 - h, R)
        return pltpu.make_async_remote_copy(
            src_ref=recv.at[where],
            dst_ref=recv.at[where],
            send_sem=send_sems.at[k],
            recv_sem=recv_sems.at[k],
            device_id={"layer": s - 1},
            device_id_type=MESH,
        )

    pl.semaphore_wait(barrier, jnp.where(s > 0, 1, 0) + jnp.where(s < sections - 1, 1, 0))

    def spread_end(j):
        at = rows(BLK * j, BLK)
        spread(z_chain, BLK * j, BLK, slopes[0, at], ends[at])

    blocks = -(-(end_row + 1) // BLK)
    spread_end(0)

    @pl.loop(0, blocks)
    def _(j):
        @pl.when(j < blocks - 1)
        def _():
            spread_end(j + 1)

        at = rows(BLK * j, BLK)
        ends[at] = ends[at] + STEP * conv(z_chain, 0, BLK * j, BLK)

        @pl.when(h == 0)
        def _():
            for q in range(Q):
                k = Q * j - 1 + q

                @pl.when((k >= 0) & sends(k, 0))
                def _():
                    chunk(ends, k).start()

    for copy in rest:
        copy.wait()

    @pl.when(h == 0)
    def _():
        for i in range(2):
            at = rows(image_row[i], height)
            recv[at] = last[at]

    def fine(j, piece):
        start = BLK * (j - 1) + 2 - jnp.maximum(h, 1)

        def gradient(layer, z, at):
            lhs = jnp.concatenate(
                [states[layer, rows(at + a - 1, BLK)].T for a in range(3)], axis=0
            )
            for b in range(3):
                term = jnp.dot(lhs, z[rows(at, BLK), b * chans:(b + 1) * chans],
                               preferred_element_type=jnp.float32)
                for a in range(3):
                    grad[layer, 3 * a + b] += term[a * chans:(a + 1) * chans]

        if piece == 0:
            at = rows(start, BLK)
            spread(z_up, start, BLK, slopes[1, at], recv[at])
            at = rows(start - 1, BLK)
            mid[at] = recv[at] + STEP * conv(z_up, 1, start - 1, BLK)
        elif piece == 1:
            at = rows(start - 1, BLK)
            spread(z_dn, start - 1, BLK, slopes[0, at], mid[at])
            at = rows(start - 2, BLK + 1)
            low[at] = mid[at] + STEP * conv(z_dn, 0, start - 2, BLK + 1)
        elif piece == 2:
            gradient(1, z_up, start)
        else:
            gradient(0, z_dn, start - 1)

    outer = -(-(end_row + sections - 2) // BLK)

    @pl.loop(0, outer)
    def _(j):
        for q in range(Q):
            k = Q * j + q
            taken = (h > 0) & sends(k, h - 1)

            @pl.when(taken)
            def _():
                arrival(k).wait_recv()

            @pl.when(taken & (s > 0))
            def _():
                at = rows(R * k + 2 - h, R)
                spread(z_chain, R * k + 2 - h, R, slopes[0, at], recv[at] - last[at])

            @pl.when((h > 0) & (s > 0) & sends(k, h))
            def _():
                at = rows(R * k + 1 - h, R)
                send[at] = ((recv[at] - last[at]) + 2 * STEP * conv(z_chain, 0, R * k + 1 - h, R)) + ends[at]
                chunk(send, k).start()

            @pl.when(j > 0)
            def _():
                fine(j, q)

    for piece in range(4):
        fine(outer, piece)

    grad[...] = grad[...] * scale
    outs = [load(image(low, i), lower_hbm.at[i], out_sems.at[i]) for i in range(2)]
    outs.append(load(grad, grad_hbm, out_sems.at[2]))

    @pl.loop(0, outer * Q)
    def _(k):
        @pl.when((s > 0) & sends(k, h))
        def _():
            chunk(send, k).wait_send()

    for copy in outs:
        copy.wait()


def on_device(states, slopes, kernels, guess):
    layers, images, height, width, chans = states.shape
    sections = lax.axis_size("layer")
    replicas = lax.axis_size("dp")
    scale = STEP / (images * replicas)
    pix = height * width
    flat = lambda array: array.reshape(layers, images, pix, chans)
    steps = Q * -(-(2 * height + 1 + sections - 2) // BLK)
    size = ROWS * width
    any_space = pl.BlockSpec(memory_space=pl.ANY)
    f32, bf16 = jnp.float32, jnp.bfloat16
    lower, grads = pl.pallas_call(
        functools.partial(chain_kernel, sections, scale, height, width, chans),
        out_shape=(
            jax.ShapeDtypeStruct((images, pix, chans), f32),
            jax.ShapeDtypeStruct((layers, 9, chans, chans), f32),
        ),
        in_specs=[any_space] * 4,
        out_specs=(any_space, any_space),
        scratch_shapes=[
            pltpu.VMEM((layers, size, chans), bf16),
            pltpu.VMEM((layers, size, chans), bf16),
            pltpu.VMEM((layers, 9, chans, chans), bf16),
            pltpu.VMEM((size, chans), f32),
            pltpu.VMEM((size, chans), f32),
            pltpu.VMEM((size, chans), f32),
            pltpu.VMEM((size, chans), f32),
            pltpu.VMEM((size, chans), f32),
            pltpu.VMEM((size, chans), f32),
            pltpu.VMEM((size, 3 * chans), bf16),
            pltpu.VMEM((size, 3 * chans), bf16),
            pltpu.VMEM((size, 3 * chans), bf16),
            pltpu.VMEM((layers, 9, chans, chans), f32),
            pltpu.SemaphoreType.DMA((14,)),
            pltpu.SemaphoreType.DMA((steps,)),
            pltpu.SemaphoreType.DMA((steps,)),
            pltpu.SemaphoreType.DMA((3,)),
        ],
        compiler_params=pltpu.CompilerParams(
            collective_id=0, has_side_effects=True, vmem_limit_bytes=60 * 1024 * 1024
        ),
    )(flat(states), flat(slopes), kernels, flat(guess))
    summed = lax.psum_scatter(grads, "dp", scatter_dimension=2, tiled=True)
    return (lower.reshape(1, images, height, width, chans), summed)


def solution(mesh):
    return jax.shard_map(
        on_device,
        mesh=mesh,
        in_specs=(
            P("layer", "dp", None, None, None),
            P("layer", "dp", None, None, None),
            P("layer", None, None, None),
            P("layer", "dp", None, None, None),
        ),
        out_specs=(P("layer", "dp", None, None, None), P("layer", None, "dp", None)),
        check_vma=False,
    )
```

time: 627 us -> 236 us (0.38)
  waiting for transfers between devices: 500 us -> 129 us
  Pallas kernels: 0 us -> 87.6 us
  other arithmetic: 45.3 us -> 0 us
  local copies, waits for them, and re-layouts: 33 us -> 1.32 us
  matrix products: 16 us -> 0 us
  starting transfers between devices: 9 us -> 0.04 us
    ppermute x7 -> x0, waiting for transfers between devices: 376 us -> none  [from_behind(): return lax.ppermute(array, axis, pairs)]
    pallas_call x0 -> x1, Pallas kernels: none -> 87.6 us  [on_device(): pl.pallas_call(functools.partial(chain_kernel, sections, scale, height, w...]
    select_n x7 -> x0, other arithmetic: 23.1 us -> none  [advance_turn(): jnp.where(position == sections - 2 - moment, arrived_top - guess_last, co...]
    dot_general x5 -> x0, matrix products: 16 us -> none  [the longest x3 9.72 us: transpose_conv(): jnp.einsum('iyxtc,tdc->iyxd', pieces, kernel, preferred_element_type=jnp....]
    unnamed x62 -> x3, local copies, waits for them, and re-layouts: 15.7 us -> 1.32 us
    another operation x12 -> x0, local copies, waits for them, and re-layouts: 13.8 us -> none
    while x7 -> x0, other arithmetic: 11.2 us -> none
    ppermute x7 -> x0, starting transfers between devices: 8.96 us -> none  [from_behind(): return lax.ppermute(array, axis, pairs)]
  transfers between devices with their start and end apart: 8 -> 1, of which waited for: 8 -> 1; matrix products, arithmetic and copies ran while one was open for 1% -> 0% of each run, Pallas kernels for 0% -> 0%
where the time goes in v1:
time: 236 us; the launch traced here: 232 us
  waiting for transfers between devices  129 us (55%)
  Pallas kernels  87.6 us (37%)
  between operations  14 us (6%)
    reduce_scatter x1, waiting for transfers between devices, on_device(): summed = lax.psum_scatter(grads, 'dp', scatter_dimension=2, tiled=True)  129 us
    pallas_call x1, Pallas kernels, on_device(): pl.pallas_call(functools.partial(chain_kernel, sections, scale, height, w...  87.6 us
  transfers between devices with their start and end apart: 1, of which 1 were waited for; matrix products, arithmetic and copies ran while one was open for 0% of the time, Pallas kernels for 0%

profile of v1, /device:TPU:1, one launch (start us, length us, event | category | flops | bytes accessed | tf_op | source)
XLA Modules:
  0.0 232.4 jit_solution(1792617367933610126)
XLA Ops:
  7.2 0.0 reduce-scatter.2.cloned.1.call-start
  7.2 87.6 %shard_map.59 = (f32[2,1024,256]{2,1,0:T(8,128)}, f32[2,9,256,256]{3,2,1,0:T(8,128)}) custom-call(bf16[2,2,1024,256]{3,2,1,0:T(8,128)(2,1)} %bitcast.6, bf16[2,2,1024,256]{3,2,1,0:T(8,128)(2,1)} %bitcast.7, bf16[2,9,256,256]{3,2,1,0:T(8,128)(2,1)} %kernels_hbm.1, f32[2,2,1024,256]{3,2,1,0:T(8,128)} %bitcast.4), custom_call_target="tpu_custom_call" | custom-call | tf_op jit(solution)/shard_map/pallas_call | solution.py:254
  94.8 0.0 copy-start
  94.8 0.0 reduce-scatter.2.cloned.1.call-update
  94.8 129.4 %reduce-scatter.2.cloned.1.call-done = f32[2,9,8,256]{3,2,1,0:T(8,128)} async-done(((f32[2,9,256,256]{3,2,1,0:T(8,128)}), f32[2,9,8,256]{3,2,1,0:T(8,128)}) %reduce-scatter.2.cloned.1.call-update) | async-done | bytes 147472 | tf_op jit(solution)/shard_map/reduce_scatter | solution.py:285
  224.2 0.0 copy-done
  224.2 1.3 copy.7
Async XLA Ops:
  7.2 217.1 %reduce-scatter.2.cloned.1.call-start = ((), (), s32[]{:S(2)}) async-start(), calls=%async_computation.1 | async-start | bytes 4866048 | tf_op jit(solution)/shard_map/reduce_scatter | solution.py:285
  94.8 129.4 %copy-start = (f32[2,1024,256]{2,1,0:T(8,128)S(1)}, f32[2,1024,256]{2,1,0:T(8,128)}, u32[]{:S(2)}) copy-start(f32[2,1024,256]{2,1,0:T(8,128)} %get-tuple-element.4) | copy-start | bytes 6291460
Sparse Core Ops, SparseCore 0:
  94.9 129.2 reduce-scatter.1

commit v2 on v1

--- a/solution.py
+++ b/solution.py
@@ -14,6 +14,7 @@
 R = 2
 Q = 4
 BLK = R * Q
+PART = 6
 
 
 def chain_kernel(
@@ -21,7 +22,9 @@
     states_hbm, slopes_hbm, kernels_hbm, guess_hbm,
     lower_hbm, grad_hbm,
     states, slopes, kern, last, ends, recv, send, mid, low, z_chain, z_up, z_dn, grad,
+    core_in, ring_in, cross_in, result,
     load_sems, send_sems, recv_sems, out_sems,
+    core_sems, ring_send, ring_recv, cross_sems,
 ):
     s = lax.axis_index("layer")
     h = sections - 1 - s
@@ -58,8 +61,20 @@
         for l in range(2):
             rest.append(load(states_hbm.at[l, i], image(states.at[l], i), load_sems.at[10 + 2 * l + i]))
 
+    place = lax.axis_index("dp")
+    ring = lax.axis_size("dp") // 4
+    depth = place // 4
+    cross = (place // 2) % 2
+    core = place % 2
+    beside = place + 1 - 2 * core
+    over = place + 2 - 4 * cross
+    after = ((depth + 1) % ring) * 4 + place % 4
+    before = ((depth + ring - 1) % ring) * 4 + place % 4
+
     clear(recv)
     barrier = pltpu.get_barrier_semaphore()
+    for peer in (beside, over, after, before):
+        pl.semaphore_signal(barrier, inc=1, device_id={"dp": peer}, device_id_type=MESH)
 
     @pl.when(s > 0)
     def _():
@@ -132,7 +147,7 @@
             device_id_type=MESH,
         )
 
-    pl.semaphore_wait(barrier, jnp.where(s > 0, 1, 0) + jnp.where(s < sections - 1, 1, 0))
+    pl.semaphore_wait(barrier, 4 + jnp.where(s > 0, 1, 0) + jnp.where(s < sections - 1, 1, 0))
 
     def spread_end(j):
         at = rows(BLK * j, BLK)
@@ -179,7 +194,8 @@
                 term = jnp.dot(lhs, z[rows(at, BLK), b * chans:(b + 1) * chans],
                                preferred_element_type=jnp.float32)
                 for a in range(3):
-                    grad[layer, 3 * a + b] += term[a * chans:(a + 1) * chans]
+                    part = term[a * chans:(a + 1) * chans]
+                    grad[9 * layer + 3 * a + b] += part.reshape(grad.shape[1:])
 
         if piece == 0:
             at = rows(start, BLK)
@@ -226,9 +242,73 @@
     for piece in range(4):
         fine(outer, piece)
 
-    grad[...] = grad[...] * scale
     outs = [load(image(low, i), lower_hbm.at[i], out_sems.at[i]) for i in range(2)]
-    outs.append(load(grad, grad_hbm, out_sems.at[2]))
+
+    def remote(src, dst, send_sem, recv_sem, peer):
+        return pltpu.make_async_remote_copy(
+            src_ref=src, dst_ref=dst, send_sem=send_sem, recv_sem=recv_sem,
+            device_id={"dp": peer}, device_id_type=MESH,
+        )
+
+    def part(u):
+        return slice(PART * u, PART * (u + 1))
+
+    parts = grad.shape[0] // PART
+    half = ring // 2
+
+    def core_copy(u):
+        return remote(grad.at[part(u), :, :, 1 - core], core_in.at[part(u)],
+                      core_sems.at[0, u], core_sems.at[1, u], beside)
+
+    def ring_copy(way, j, u):
+        away = half - j
+        target = (depth + away) % ring if way == 0 else (depth + ring - away) % ring
+        src, dst = grad.at[part(u), target, :, core], ring_in.at[way, j, part(u)]
+        if j == 0:
+            src, dst = src.at[:, way], dst.at[:, way]
+        return remote(src, dst, ring_send.at[way, j, u], ring_recv.at[way, j, u],
+                      after if way == 0 else before)
+
+    def cross_copy(u):
+        return remote(grad.at[part(u), depth, 1 - cross, core], cross_in.at[part(u)],
+                      cross_sems.at[0, u], cross_sems.at[1, u], over)
+
+    def add_arrived(way, j, u):
+        ring_copy(way, j, u).wait_recv()
+        away = half - 1 - j
+        target = (depth + away) % ring if way == 0 else (depth + ring - away) % ring
+        if j == 0:
+            grad[part(u), target, way, core] += ring_in[way, j, part(u), way]
+        else:
+            grad[part(u), target, :, core] += ring_in[way, j, part(u)]
+
+    for u in range(parts):
+        core_copy(u).start()
+    for u in range(parts):
+        core_copy(u).wait_recv()
+        grad[part(u), :, :, core] += core_in[part(u)]
+        for way in range(2):
+            ring_copy(way, 0, u).start()
+    for j in range(1, half):
+        for u in range(parts):
+            for way in range(2):
+                add_arrived(way, j - 1, u)
+                ring_copy(way, j, u).start()
+    for u in range(parts):
+        for way in range(2):
+            add_arrived(way, half - 1, u)
+        cross_copy(u).start()
+    for u in range(parts):
+        cross_copy(u).wait_recv()
+        result[part(u)] = (grad[part(u), depth, cross, core] + cross_in[part(u)]) * scale
+    outs.append(load(result, grad_hbm, out_sems.at[2]))
+
+    for u in range(parts):
+        core_copy(u).wait_send()
+        cross_copy(u).wait_send()
+        for j in range(half):
+            for way in range(2):
+                ring_copy(way, j, u).wait_send()
 
     @pl.loop(0, outer * Q)
     def _(k):
@@ -251,11 +331,13 @@
     size = ROWS * width
     any_space = pl.BlockSpec(memory_space=pl.ANY)
     f32, bf16 = jnp.float32, jnp.bfloat16
+    ring = replicas // 4
+    share = chans // replicas
     lower, grads = pl.pallas_call(
         functools.partial(chain_kernel, sections, scale, height, width, chans),
         out_shape=(
             jax.ShapeDtypeStruct((images, pix, chans), f32),
-            jax.ShapeDtypeStruct((layers, 9, chans, chans), f32),
+            jax.ShapeDtypeStruct((layers * 9, chans // replicas, chans), f32),
         ),
         in_specs=[any_space] * 4,
         out_specs=(any_space, any_space),
@@ -272,18 +354,28 @@
             pltpu.VMEM((size, 3 * chans), bf16),
             pltpu.VMEM((size, 3 * chans), bf16),
             pltpu.VMEM((size, 3 * chans), bf16),
-            pltpu.VMEM((layers, 9, chans, chans), f32),
+            pltpu.VMEM((layers * 9, ring, 2, 2, share, chans), f32),
+            pltpu.VMEM((layers * 9, ring, 2, share, chans), f32),
+            pltpu.VMEM((2, ring // 2, layers * 9, 2, share, chans), f32),
+            pltpu.VMEM((layers * 9, share, chans), f32),
+            pltpu.VMEM((layers * 9, share, chans), f32),
             pltpu.SemaphoreType.DMA((14,)),
             pltpu.SemaphoreType.DMA((steps,)),
             pltpu.SemaphoreType.DMA((steps,)),
             pltpu.SemaphoreType.DMA((3,)),
+            pltpu.SemaphoreType.DMA((2, layers * 9 // PART)),
+            pltpu.SemaphoreType.DMA((2, ring // 2, layers * 9 // PART)),
+            pltpu.SemaphoreType.DMA((2, ring // 2, layers * 9 // PART)),
+            pltpu.SemaphoreType.DMA((2, layers * 9 // PART)),
         ],
         compiler_params=pltpu.CompilerParams(
             collective_id=0, has_side_effects=True, vmem_limit_bytes=60 * 1024 * 1024
         ),
     )(flat(states), flat(slopes), kernels, flat(guess))
-    summed = lax.psum_scatter(grads, "dp", scatter_dimension=2, tiled=True)
-    return (lower.reshape(1, images, height, width, chans), summed)
+    return (
+        lower.reshape(1, images, height, width, chans),
+        grads.reshape(layers, 9, share, chans),
+    )
 
 
 def solution(mesh):

time: 236 us -> 128 us (0.54); the launches traced: 232 us -> 128 us
  waiting for transfers between devices: 129 us -> 0 us
  Pallas kernels: 87.6 us -> 123 us
  between operations: 14 us -> 0.65 us
  local copies, waits for them, and re-layouts: 1.32 us -> 3.86 us
    reduce_scatter x1 -> x0, waiting for transfers between devices: 129 us -> none  [on_device(): summed = lax.psum_scatter(grads, 'dp', scatter_dimension=2, tiled=True)]
    pallas_call x1, Pallas kernels: 87.6 us -> 123 us  [on_device(): pl.pallas_call(functools.partial(chain_kernel, sections, scale, height, w...]
    unnamed x3 -> x4, local copies, waits for them, and re-layouts: 1.32 us -> 3.86 us
  transfers between devices with their start and end apart: 1 -> 0, of which waited for: 1 -> 0; matrix products, arithmetic and copies ran while one was open for 0% -> 0% of each run, Pallas kernels for 0% -> 0%
where the time goes in v2:
time: 128 us
  Pallas kernels  123 us (96%)
  local copies, waits for them, and re-layouts  3.86 us (3%)
    pallas_call x1, Pallas kernels, on_device(): pl.pallas_call(functools.partial(chain_kernel, sections, scale, height, w...  123 us
    unnamed x4, local copies, waits for them, and re-layouts  3.86 us

profile of v2, /device:TPU:1, one launch (start us, length us, event | category | flops | bytes accessed | tf_op | source)
XLA Modules:
  0.0 128.0 jit_solution(14569090179907731477)
XLA Ops:
  0.6 123.5 %shard_map.59 = (f32[2,1024,256]{2,1,0:T(8,128)}, f32[18,8,256]{2,1,0:T(8,128)}) custom-call(bf16[2,2,1024,256]{3,2,1,0:T(8,128)(2,1)} %bitcast.7, bf16[2,2,1024,256]{3,2,1,0:T(8,128)(2,1)} %bitcast.8, bf16[2,9,256,256]{3,2,1,0:T(8,128)(2,1)} %kernels_hbm.1, f32[2,2,1024,256]{3,2,1,0:T(8,128)} %bitcast.5), custom_call_target="tpu_custom_call" | custom-call | tf_op jit(solution)/shard_map/pallas_call | solution.py:336
  124.1 0.0 copy-start
  124.1 3.2 %copy.8 = f32[1,2,32,32,256]{4,3,2,1,0:T(8,128)} copy(f32[1,2,32,32,256]{4,3,2,1,0:T(8,128)} %bitcast.6) | data formatting | bytes 4194304
  127.3 0.0 copy-done
  127.3 0.7 copy.9
Async XLA Ops:
  124.1 3.2 %copy-start = (f32[18,8,256]{2,1,0:T(8,128)S(1)}, f32[18,8,256]{2,1,0:T(8,128)}, u32[]{:S(2)}) copy-start(f32[18,8,256]{2,1,0:T(8,128)} %get-tuple-element.5) | copy-start | bytes 442372

commit v3 on v2

--- a/solution.py
+++ b/solution.py
@@ -14,7 +14,9 @@
 R = 2
 Q = 4
 BLK = R * Q
-PART = 6
+PART = 3
+RING_FIRST = (3, 0, 1, 2)
+CROSS_FIRST = (4, 5)
 
 
 def chain_kernel(
@@ -22,7 +24,7 @@
     states_hbm, slopes_hbm, kernels_hbm, guess_hbm,
     lower_hbm, grad_hbm,
     states, slopes, kern, last, ends, recv, send, mid, low, z_chain, z_up, z_dn, grad,
-    core_in, ring_in, cross_in, result,
+    core_in, ring_in, cross_in, wide_in, result,
     load_sems, send_sems, recv_sems, out_sems,
     core_sems, ring_send, ring_recv, cross_sems,
 ):
@@ -54,13 +56,6 @@
     for i in range(2):
         first.append(load(guess_hbm.at[0, i], image(ends, i), load_sems.at[1 + i]))
         first.append(load(slopes_hbm.at[0, i], image(slopes.at[0], i), load_sems.at[3 + i]))
-    rest = [load(kernels_hbm.at[1], kern.at[1], load_sems.at[5])]
-    for i in range(2):
-        rest.append(load(guess_hbm.at[1, i], image(last, i), load_sems.at[6 + i]))
-        rest.append(load(slopes_hbm.at[1, i], image(slopes.at[1], i), load_sems.at[8 + i]))
-        for l in range(2):
-            rest.append(load(states_hbm.at[l, i], image(states.at[l], i), load_sems.at[10 + 2 * l + i]))
-
     place = lax.axis_index("dp")
     ring = lax.axis_size("dp") // 4
     depth = place // 4
@@ -96,8 +91,14 @@
     z_dn[rows(-TOP, TOP + 4)] = jnp.zeros(((TOP + 4) * width, 3 * chans), jnp.bfloat16)
     grad[...] = jnp.zeros(grad.shape, jnp.float32)
 
-    for copy in first:
+    for copy in first[:3]:
         copy.wait()
+    rest = [load(kernels_hbm.at[1], kern.at[1], load_sems.at[5])]
+    for i in range(2):
+        rest.append(load(guess_hbm.at[1, i], image(last, i), load_sems.at[6 + i]))
+        rest.append(load(slopes_hbm.at[1, i], image(slopes.at[1], i), load_sems.at[8 + i]))
+        for l in range(2):
+            rest.append(load(states_hbm.at[l, i], image(states.at[l], i), load_sems.at[10 + 2 * l + i]))
 
     def spread(z, start, count, slope, values):
         cot = slope.astype(jnp.float32) * values
@@ -121,12 +122,12 @@
                 total = term if total is None else total + term
         return total
 
-    def sends(k, hop):
-        start = R * k + 1 - hop
-        return (start + R - 1 >= 1) & (start <= end_row)
-
-    def chunk(src, k):
-        where = rows(R * k + 1 - h, R)
+    def sends(base, size, hop):
+        start = base + 1 - hop
+        return (start + size - 1 >= 1) & (start <= end_row)
+
+    def chunk(src, k, base, size):
+        where = rows(base + 1 - h, size)
         return pltpu.make_async_remote_copy(
             src_ref=src.at[where],
             dst_ref=recv.at[where],
@@ -136,8 +137,8 @@
             device_id_type=MESH,
         )
 
-    def arrival(k):
-        where = rows(R * k + 2 - h, R)
+    def arrival(k, base, size):
+        where = rows(base + 2 - h, size)
         return pltpu.make_async_remote_copy(
             src_ref=recv.at[where],
             dst_ref=recv.at[where],
@@ -147,17 +148,21 @@
             device_id_type=MESH,
         )
 
-    pl.semaphore_wait(barrier, 4 + jnp.where(s > 0, 1, 0) + jnp.where(s < sections - 1, 1, 0))
-
     def spread_end(j):
         at = rows(BLK * j, BLK)
         spread(z_chain, BLK * j, BLK, slopes[0, at], ends[at])
 
     blocks = -(-(end_row + 1) // BLK)
+    coarse = (end_row - 1) // BLK
     spread_end(0)
 
     @pl.loop(0, blocks)
     def _(j):
+        @pl.when(j == image_row[1] // BLK - 1)
+        def _():
+            for copy in first[3:]:
+                copy.wait()
+
         @pl.when(j < blocks - 1)
         def _():
             spread_end(j + 1)
@@ -165,14 +170,23 @@
         at = rows(BLK * j, BLK)
         ends[at] = ends[at] + STEP * conv(z_chain, 0, BLK * j, BLK)
 
-        @pl.when(h == 0)
+        @pl.when(j == 0)
+        def _():
+            peers = 4 + jnp.where(s > 0, 1, 0) + jnp.where(s < sections - 1, 1, 0)
+            pl.semaphore_wait(barrier, peers)
+
+        @pl.when((h == 0) & (s > 0))
         def _():
             for q in range(Q):
                 k = Q * j - 1 + q
 
-                @pl.when((k >= 0) & sends(k, 0))
+                @pl.when((k >= 0) & (k < Q * coarse))
                 def _():
-                    chunk(ends, k).start()
+                    chunk(ends, k, R * k, R).start()
+
+    @pl.when((h == 0) & (s > 0))
+    def _():
+        chunk(ends, Q * coarse, BLK * coarse, 1).start()
 
     for copy in rest:
         copy.wait()
@@ -212,37 +226,37 @@
         else:
             gradient(0, z_dn, start - 1)
 
-    outer = -(-(end_row + sections - 2) // BLK)
-
-    @pl.loop(0, outer)
+    def step(k, base, size):
+        taken = (h > 0) & sends(base, size, h - 1)
+
+        @pl.when(taken)
+        def _():
+            arrival(k, base, size).wait_recv()
+
+        @pl.when(taken & (s > 0))
+        def _():
+            at = rows(base + 2 - h, size)
+            spread(z_chain, base + 2 - h, size, slopes[0, at], recv[at] - last[at])
+
+        @pl.when((h > 0) & (s > 0) & sends(base, size, h))
+        def _():
+            at = rows(base + 1 - h, size)
+            send[at] = ((recv[at] - last[at]) + 2 * STEP * conv(z_chain, 0, base + 1 - h, size)) + ends[at]
+            chunk(send, k, base, size).start()
+
+    @pl.loop(0, coarse)
     def _(j):
         for q in range(Q):
-            k = Q * j + q
-            taken = (h > 0) & sends(k, h - 1)
-
-            @pl.when(taken)
-            def _():
-                arrival(k).wait_recv()
-
-            @pl.when(taken & (s > 0))
-            def _():
-                at = rows(R * k + 2 - h, R)
-                spread(z_chain, R * k + 2 - h, R, slopes[0, at], recv[at] - last[at])
-
-            @pl.when((h > 0) & (s > 0) & sends(k, h))
-            def _():
-                at = rows(R * k + 1 - h, R)
-                send[at] = ((recv[at] - last[at]) + 2 * STEP * conv(z_chain, 0, R * k + 1 - h, R)) + ends[at]
-                chunk(send, k).start()
+            step(Q * j + q, BLK * j + R * q, R)
 
             @pl.when(j > 0)
             def _():
                 fine(j, q)
 
-    for piece in range(4):
-        fine(outer, piece)
-
-    outs = [load(image(low, i), lower_hbm.at[i], out_sems.at[i]) for i in range(2)]
+    for i in range(BLK):
+        step(Q * coarse + i, BLK * coarse + i, 1)
+        if i % 2 == 1:
+            fine(coarse, i // 2)
 
     def remote(src, dst, send_sem, recv_sem, peer):
         return pltpu.make_async_remote_copy(
@@ -260,45 +274,86 @@
         return remote(grad.at[part(u), :, :, 1 - core], core_in.at[part(u)],
                       core_sems.at[0, u], core_sems.at[1, u], beside)
 
+    def ring_target(way, away):
+        return (depth + away) % ring if way == 0 else (depth + ring - away) % ring
+
+    def carries(way, j, u):
+        return u in RING_FIRST or j > 0 or way == u % 2
+
     def ring_copy(way, j, u):
-        away = half - j
-        target = (depth + away) % ring if way == 0 else (depth + ring - away) % ring
-        src, dst = grad.at[part(u), target, :, core], ring_in.at[way, j, part(u)]
-        if j == 0:
-            src, dst = src.at[:, way], dst.at[:, way]
+        target = ring_target(way, half - j)
+        if u in CROSS_FIRST:
+            src, dst = grad.at[part(u), target, cross, core], ring_in.at[way, j, part(u), 0]
+        elif j == 0:
+            src, dst = grad.at[part(u), target, way, core], ring_in.at[way, j, part(u), way]
+        else:
+            src, dst = grad.at[part(u), target, :, core], ring_in.at[way, j, part(u)]
         return remote(src, dst, ring_send.at[way, j, u], ring_recv.at[way, j, u],
                       after if way == 0 else before)
 
-    def cross_copy(u):
-        return remote(grad.at[part(u), depth, 1 - cross, core], cross_in.at[part(u)],
-                      cross_sems.at[0, u], cross_sems.at[1, u], over)
-
     def add_arrived(way, j, u):
+        if not carries(way, j, u):
+            return
         ring_copy(way, j, u).wait_recv()
-        away = half - 1 - j
-        target = (depth + away) % ring if way == 0 else (depth + ring - away) % ring
-        if j == 0:
+        target = ring_target(way, half - 1 - j)
+        if u in CROSS_FIRST:
+            grad[part(u), target, cross, core] += ring_in[way, j, part(u), 0]
+        elif j == 0:
             grad[part(u), target, way, core] += ring_in[way, j, part(u), way]
         else:
             grad[part(u), target, :, core] += ring_in[way, j, part(u)]
 
-    for u in range(parts):
+    def ring_round(j, pieces):
+        for u in pieces:
+            for way in range(2):
+                if j > 0:
+                    add_arrived(way, j - 1, u)
+                if j < half and carries(way, j, u):
+                    ring_copy(way, j, u).start()
+
+    def wide_part(u):
+        first_tap = PART * (u - CROSS_FIRST[0])
+        return slice(first_tap, first_tap + PART)
+
+    def cross_copy(u):
+        if u in CROSS_FIRST:
+            src, dst = grad.at[part(u), :, 1 - cross, core], wide_in.at[wide_part(u)]
+        else:
+            src, dst = grad.at[part(u), depth, 1 - cross, core], cross_in.at[part(u)]
+        return remote(src, dst, cross_sems.at[0, u], cross_sems.at[1, u], over)
+
+    fine(coarse + 1, 0)
+    fine(coarse + 1, 2)
+    for u in CROSS_FIRST + RING_FIRST[:1]:
         core_copy(u).start()
-    for u in range(parts):
+    fine(coarse + 1, 1)
+    fine(coarse + 1, 3)
+    for u in RING_FIRST[1:]:
+        core_copy(u).start()
+    outs = [load(image(low, i), lower_hbm.at[i], out_sems.at[i]) for i in range(2)]
+
+    for u in CROSS_FIRST + RING_FIRST:
         core_copy(u).wait_recv()
         grad[part(u), :, :, core] += core_in[part(u)]
-        for way in range(2):
-            ring_copy(way, 0, u).start()
-    for j in range(1, half):
-        for u in range(parts):
-            for way in range(2):
-                add_arrived(way, j - 1, u)
-                ring_copy(way, j, u).start()
-    for u in range(parts):
-        for way in range(2):
-            add_arrived(way, half - 1, u)
-        cross_copy(u).start()
-    for u in range(parts):
+        if u in CROSS_FIRST:
+            cross_copy(u).start()
+        else:
+            ring_round(0, (u,))
+    ring_round(1, RING_FIRST)
+    for u in CROSS_FIRST:
+        cross_copy(u).wait_recv()
+        grad[part(u), :, cross, core] += wide_in[wide_part(u)]
+    ring_round(0, CROSS_FIRST)
+    for j in range(2, half + 1):
+        ring_round(j, RING_FIRST)
+        if j == half:
+            for u in RING_FIRST:
+                cross_copy(u).start()
+        ring_round(j - 1, CROSS_FIRST)
+    ring_round(half, CROSS_FIRST)
+    for u in CROSS_FIRST:
+        result[part(u)] = grad[part(u), depth, cross, core] * scale
+    for u in RING_FIRST:
         cross_copy(u).wait_recv()
         result[part(u)] = (grad[part(u), depth, cross, core] + cross_in[part(u)]) * scale
     outs.append(load(result, grad_hbm, out_sems.at[2]))
@@ -308,15 +363,35 @@
         cross_copy(u).wait_send()
         for j in range(half):
             for way in range(2):
-                ring_copy(way, j, u).wait_send()
-
-    @pl.loop(0, outer * Q)
+                if carries(way, j, u):
+                    ring_copy(way, j, u).wait_send()
+
+    @pl.loop(0, Q * coarse)
     def _(k):
-        @pl.when((s > 0) & sends(k, h))
-        def _():
-            chunk(send, k).wait_send()
+        @pl.when((s > 0) & sends(R * k, R, h))
+        def _():
+            chunk(send, k, R * k, R).wait_send()
+
+    for i in range(BLK):
+        @pl.when((s > 0) & sends(BLK * coarse + i, 1, h))
+        def _():
+            chunk(send, Q * coarse + i, BLK * coarse + i, 1).wait_send()
 
     for copy in outs:
+        copy.wait()
+
+
+def deliver(lower_in, grads_in, lower_out, grads_out, sems):
+    copies = [pltpu.make_async_copy(grads_in, grads_out, sems.at[0])]
+    size = lower_in.shape[1] // 4
+    for i in range(lower_in.shape[0]):
+        for j in range(4):
+            where = pl.ds(size * j, size)
+            copies.append(pltpu.make_async_copy(
+                lower_in.at[i, where], lower_out.at[i, where], sems.at[1 + 4 * i + j]))
+    for copy in copies:
+        copy.start()
+    for copy in copies:
         copy.wait()
 
 
@@ -327,7 +402,7 @@
     scale = STEP / (images * replicas)
     pix = height * width
     flat = lambda array: array.reshape(layers, images, pix, chans)
-    steps = Q * -(-(2 * height + 1 + sections - 2) // BLK)
+    steps = Q * (2 * height // BLK) + BLK
     size = ROWS * width
     any_space = pl.BlockSpec(memory_space=pl.ANY)
     f32, bf16 = jnp.float32, jnp.bfloat16
@@ -358,6 +433,7 @@
             pltpu.VMEM((layers * 9, ring, 2, share, chans), f32),
             pltpu.VMEM((2, ring // 2, layers * 9, 2, share, chans), f32),
             pltpu.VMEM((layers * 9, share, chans), f32),
+            pltpu.VMEM((len(CROSS_FIRST) * PART, ring, share, chans), f32),
             pltpu.VMEM((layers * 9, share, chans), f32),
             pltpu.SemaphoreType.DMA((14,)),
             pltpu.SemaphoreType.DMA((steps,)),
@@ -372,6 +448,16 @@
             collective_id=0, has_side_effects=True, vmem_limit_bytes=60 * 1024 * 1024
         ),
     )(flat(states), flat(slopes), kernels, flat(guess))
+    lower, grads = pl.pallas_call(
+        deliver,
+        out_shape=(
+            jax.ShapeDtypeStruct(lower.shape, f32),
+            jax.ShapeDtypeStruct(grads.shape, f32),
+        ),
+        in_specs=[any_space] * 2,
+        out_specs=(any_space, any_space),
+        scratch_shapes=[pltpu.SemaphoreType.DMA((1 + 4 * images,))],
+    )(lower, grads)
     return (
         lower.reshape(1, images, height, width, chans),
         grads.reshape(layers, 9, share, chans),

time: 128 us -> 192 us (1.50)
  Pallas kernels: 123 us -> 191 us
  local copies, waits for them, and re-layouts: 3.86 us -> 0 us
    pallas_call x0 -> x1, Pallas kernels: none -> 69.2 us  [on_device(): pl.pallas_call(deliver, out_shape=(jax.ShapeDtypeStruct(lower.shape, f32)...]
    unnamed x4 -> x0, local copies, waits for them, and re-layouts: 3.86 us -> none
where the time goes in v3:
time: 192 us; the launch traced here: 191 us
  Pallas kernels  191 us (99%)
    pallas_call x1, Pallas kernels, on_device(): pl.pallas_call(functools.partial(chain_kernel, sections, scale, height, w...  122 us
    pallas_call x1, Pallas kernels, on_device(): pl.pallas_call(deliver, out_shape=(jax.ShapeDtypeStruct(lower.shape, f32)...  69.2 us

profile of v3, /device:TPU:1, one launch (start us, length us, event | category | flops | bytes accessed | tf_op | source)
XLA Modules:
  0.0 191.5 jit_solution(5829714633774635665)
XLA Ops:
  0.6 121.7 %shard_map.59 = (f32[2,1024,256]{2,1,0:T(8,128)}, f32[18,8,256]{2,1,0:T(8,128)}) custom-call(bf16[2,2,1024,256]{3,2,1,0:T(8,128)(2,1)} %bitcast.6, bf16[2,2,1024,256]{3,2,1,0:T(8,128)(2,1)} %bitcast.7, bf16[2,9,256,256]{3,2,1,0:T(8,128)(2,1)} %kernels_hbm.1, f32[2,2,1024,256]{3,2,1,0:T(8,128)} %bitcast.5), custom_call_target="tpu_custom_call" | custom-call | tf_op jit(solution)/shard_map/pallas_call | solution.py:411
  122.3 69.2 %shard_map.60 = (f32[2,1024,256]{2,1,0:T(8,128)}, f32[18,8,256]{2,1,0:T(8,128)}) custom-call(f32[2,1024,256]{2,1,0:T(8,128)} %get-tuple-element.6.lower_in, f32[18,8,256]{2,1,0:T(8,128)} %get-tuple-element.7.grads_in), custom_call_target="tpu_custom_call" | custom-call | tf_op jit(solution)/shard_map/pallas_call | solution.py:451

commit v4 on v3

--- a/solution.py
+++ b/solution.py
@@ -23,10 +23,10 @@
     sections, scale, height, width, chans,
     states_hbm, slopes_hbm, kernels_hbm, guess_hbm,
     lower_hbm, grad_hbm,
-    states, slopes, kern, last, ends, recv, send, mid, low, z_chain, z_up, z_dn, grad,
+    states, slopes, kern, kern_t, last, ends, recv, send, mid, low, z_chain, z_up, z_dn, grad,
     core_in, ring_in, cross_in, wide_in, result,
     load_sems, send_sems, recv_sems, out_sems,
-    core_sems, ring_send, ring_recv, cross_sems,
+    core_sems, ring_send, ring_recv, cross_sems, wide_sems,
 ):
     s = lax.axis_index("layer")
     h = sections - 1 - s
@@ -113,21 +113,22 @@
     def conv(z, layer, start, count):
         total = None
         for a in range(3):
+            term = jnp.dot(z[rows(start + 1 - a, count), :], kern_t[layer, a],
+                           preferred_element_type=jnp.float32)
+            total = term if total is None else total + term
+        return total
+
+    def turn(layer):
+        for a in range(3):
             for b in range(3):
-                piece = z[rows(start + 1 - a, count), b * chans:(b + 1) * chans]
-                term = lax.dot_general(
-                    piece, kern[layer, 3 * a + b], (((1,), (1,)), ((), ())),
-                    preferred_element_type=jnp.float32,
-                )
-                total = term if total is None else total + term
-        return total
+                kern_t[layer, a, b * chans:(b + 1) * chans] = kern[layer, 3 * a + b].T
 
     def sends(base, size, hop):
         start = base + 1 - hop
         return (start + size - 1 >= 1) & (start <= end_row)
 
-    def chunk(src, k, base, size):
-        where = rows(base + 1 - h, size)
+    def chunk(src, k, start, size):
+        where = rows(start, size)
         return pltpu.make_async_remote_copy(
             src_ref=src.at[where],
             dst_ref=recv.at[where],
@@ -137,16 +138,33 @@
             device_id_type=MESH,
         )
 
-    def arrival(k, base, size):
-        where = rows(base + 2 - h, size)
-        return pltpu.make_async_remote_copy(
-            src_ref=recv.at[where],
-            dst_ref=recv.at[where],
-            send_sem=send_sems.at[k],
-            recv_sem=recv_sems.at[k],
-            device_id={"layer": s - 1},
-            device_id_type=MESH,
-        )
+    def each_chunk(start, size, act):
+        if size == 1:
+            act(start, 1)
+            return
+        skip_first = (start == 0) | (start == height + 1)
+        skip_last = start == height
+
+        @pl.when(jnp.logical_not(skip_first | skip_last))
+        def _():
+            act(start, size)
+
+        @pl.when(skip_first)
+        def _():
+            act(start + 1, size - 1)
+
+        @pl.when(skip_last)
+        def _():
+            act(start, size - 1)
+
+    def start_chunk(src, k, base, size):
+        each_chunk(base + 1 - h, size, lambda at, count: chunk(src, k, at, count).start())
+
+    def sent_chunk(k, base, size):
+        each_chunk(base + 1 - h, size, lambda at, count: chunk(send, k, at, count).wait_send())
+
+    def arrived_chunk(k, base, size):
+        each_chunk(base + 2 - h, size, lambda at, count: chunk(recv, k, at, count).wait_recv())
 
     def spread_end(j):
         at = rows(BLK * j, BLK)
@@ -154,6 +172,7 @@
 
     blocks = -(-(end_row + 1) // BLK)
     coarse = (end_row - 1) // BLK
+    turn(0)
     spread_end(0)
 
     @pl.loop(0, blocks)
@@ -182,14 +201,15 @@
 
                 @pl.when((k >= 0) & (k < Q * coarse))
                 def _():
-                    chunk(ends, k, R * k, R).start()
+                    start_chunk(ends, k, R * k, R)
 
     @pl.when((h == 0) & (s > 0))
     def _():
-        chunk(ends, Q * coarse, BLK * coarse, 1).start()
+        start_chunk(ends, Q * coarse, BLK * coarse, 1)
 
     for copy in rest:
         copy.wait()
+    turn(1)
 
     @pl.when(h == 0)
     def _():
@@ -209,7 +229,9 @@
                                preferred_element_type=jnp.float32)
                 for a in range(3):
                     part = term[a * chans:(a + 1) * chans]
-                    grad[9 * layer + 3 * a + b] += part.reshape(grad.shape[1:])
+                    part = part.reshape(grad.shape[2:4] + (2,) + grad.shape[4:])
+                    for c in range(2):
+                        grad[c, 9 * layer + 3 * a + b] += part[:, :, c]
 
         if piece == 0:
             at = rows(start, BLK)
@@ -231,7 +253,7 @@
 
         @pl.when(taken)
         def _():
-            arrival(k, base, size).wait_recv()
+            arrived_chunk(k, base, size)
 
         @pl.when(taken & (s > 0))
         def _():
@@ -242,7 +264,7 @@
         def _():
             at = rows(base + 1 - h, size)
             send[at] = ((recv[at] - last[at]) + 2 * STEP * conv(z_chain, 0, base + 1 - h, size)) + ends[at]
-            chunk(send, k, base, size).start()
+            start_chunk(send, k, base, size)
 
     @pl.loop(0, coarse)
     def _(j):
@@ -267,11 +289,12 @@
     def part(u):
         return slice(PART * u, PART * (u + 1))
 
-    parts = grad.shape[0] // PART
+    parts = grad.shape[1] // PART
     half = ring // 2
+    slices = [half] + [sign * away for away in range(half - 1, 0, -1) for sign in (1, -1)] + [0]
 
     def core_copy(u):
-        return remote(grad.at[part(u), :, :, 1 - core], core_in.at[part(u)],
+        return remote(grad.at[1 - core, part(u)], core_in.at[part(u)],
                       core_sems.at[0, u], core_sems.at[1, u], beside)
 
     def ring_target(way, away):
@@ -283,11 +306,11 @@
     def ring_copy(way, j, u):
         target = ring_target(way, half - j)
         if u in CROSS_FIRST:
-            src, dst = grad.at[part(u), target, cross, core], ring_in.at[way, j, part(u), 0]
+            src, dst = grad.at[core, part(u), target, cross], ring_in.at[way, j, part(u), 0]
         elif j == 0:
-            src, dst = grad.at[part(u), target, way, core], ring_in.at[way, j, part(u), way]
+            src, dst = grad.at[core, part(u), target, way], ring_in.at[way, j, part(u), way]
         else:
-            src, dst = grad.at[part(u), target, :, core], ring_in.at[way, j, part(u)]
+            src, dst = grad.at[core, part(u), target], ring_in.at[way, j, part(u)]
         return remote(src, dst, ring_send.at[way, j, u], ring_recv.at[way, j, u],
                       after if way == 0 else before)
 
@@ -297,14 +320,18 @@
         ring_copy(way, j, u).wait_recv()
         target = ring_target(way, half - 1 - j)
         if u in CROSS_FIRST:
-            grad[part(u), target, cross, core] += ring_in[way, j, part(u), 0]
+            grad[core, part(u), target, cross] += ring_in[way, j, part(u), 0]
         elif j == 0:
-            grad[part(u), target, way, core] += ring_in[way, j, part(u), way]
+            grad[core, part(u), target, way] += ring_in[way, j, part(u), way]
         else:
-            grad[part(u), target, :, core] += ring_in[way, j, part(u)]
+            grad[core, part(u), target] += ring_in[way, j, part(u)]
 
     def ring_round(j, pieces):
         for u in pieces:
+            if u in CROSS_FIRST:
+                for n, away in enumerate(slices):
+                    if abs(away) == half - j:
+                        add_wide(u, n)
             for way in range(2):
                 if j > 0:
                     add_arrived(way, j - 1, u)
@@ -316,15 +343,24 @@
         return slice(first_tap, first_tap + PART)
 
     def cross_copy(u):
-        if u in CROSS_FIRST:
-            src, dst = grad.at[part(u), :, 1 - cross, core], wide_in.at[wide_part(u)]
-        else:
-            src, dst = grad.at[part(u), depth, 1 - cross, core], cross_in.at[part(u)]
-        return remote(src, dst, cross_sems.at[0, u], cross_sems.at[1, u], over)
+        return remote(grad.at[core, part(u), depth, 1 - cross], cross_in.at[part(u)],
+                      cross_sems.at[0, u], cross_sems.at[1, u], over)
+
+    def wide_copy(u, n):
+        target = (depth + slices[n]) % ring
+        return remote(grad.at[core, part(u), target, 1 - cross], wide_in.at[wide_part(u), n],
+                      wide_sems.at[0, u - CROSS_FIRST[0], n],
+                      wide_sems.at[1, u - CROSS_FIRST[0], n], over)
+
+    def add_wide(u, n):
+        wide_copy(u, n).wait_recv()
+        target = (depth + slices[n]) % ring
+        grad[core, part(u), target, cross] += wide_in[wide_part(u), n]
 
     fine(coarse + 1, 0)
     fine(coarse + 1, 2)
-    for u in CROSS_FIRST + RING_FIRST[:1]:
+    early = RING_FIRST[:1] + CROSS_FIRST
+    for u in early:
         core_copy(u).start()
     fine(coarse + 1, 1)
     fine(coarse + 1, 3)
@@ -332,17 +368,15 @@
         core_copy(u).start()
     outs = [load(image(low, i), lower_hbm.at[i], out_sems.at[i]) for i in range(2)]
 
-    for u in CROSS_FIRST + RING_FIRST:
+    for u in early + RING_FIRST[1:]:
         core_copy(u).wait_recv()
-        grad[part(u), :, :, core] += core_in[part(u)]
+        grad[core, part(u)] += core_in[part(u)]
         if u in CROSS_FIRST:
-            cross_copy(u).start()
+            for n in range(ring):
+                wide_copy(u, n).start()
         else:
             ring_round(0, (u,))
     ring_round(1, RING_FIRST)
-    for u in CROSS_FIRST:
-        cross_copy(u).wait_recv()
-        grad[part(u), :, cross, core] += wide_in[wide_part(u)]
     ring_round(0, CROSS_FIRST)
     for j in range(2, half + 1):
         ring_round(j, RING_FIRST)
@@ -350,48 +384,62 @@
             for u in RING_FIRST:
                 cross_copy(u).start()
         ring_round(j - 1, CROSS_FIRST)
-    ring_round(half, CROSS_FIRST)
-    for u in CROSS_FIRST:
-        result[part(u)] = grad[part(u), depth, cross, core] * scale
-    for u in RING_FIRST:
-        cross_copy(u).wait_recv()
-        result[part(u)] = (grad[part(u), depth, cross, core] + cross_in[part(u)]) * scale
-    outs.append(load(result, grad_hbm, out_sems.at[2]))
-
     for u in range(parts):
         core_copy(u).wait_send()
-        cross_copy(u).wait_send()
+        if u in CROSS_FIRST:
+            for n in range(ring):
+                wide_copy(u, n).wait_send()
         for j in range(half):
             for way in range(2):
-                if carries(way, j, u):
+                if carries(way, j, u) and (u in RING_FIRST or j < half - 1):
                     ring_copy(way, j, u).wait_send()
+    for copy in outs:
+        copy.wait()
 
     @pl.loop(0, Q * coarse)
     def _(k):
         @pl.when((s > 0) & sends(R * k, R, h))
         def _():
-            chunk(send, k, R * k, R).wait_send()
+            sent_chunk(k, R * k, R)
 
     for i in range(BLK):
         @pl.when((s > 0) & sends(BLK * coarse + i, 1, h))
         def _():
-            chunk(send, Q * coarse + i, BLK * coarse + i, 1).wait_send()
-
+            sent_chunk(Q * coarse + i, BLK * coarse + i, 1)
+
+    ring_round(half, CROSS_FIRST)
+    for u in CROSS_FIRST:
+        result[part(u)] = grad[core, part(u), depth, cross] * scale
+    for u in RING_FIRST:
+        cross_copy(u).wait_recv()
+        result[part(u)] = (grad[core, part(u), depth, cross] + cross_in[part(u)]) * scale
+    outs = [load(result, grad_hbm, out_sems.at[2])]
+
+    for u in range(parts):
+        if u in CROSS_FIRST:
+            for way in range(2):
+                ring_copy(way, half - 1, u).wait_send()
+        else:
+            cross_copy(u).wait_send()
     for copy in outs:
         copy.wait()
 
 
-def deliver(lower_in, grads_in, lower_out, grads_out, sems):
-    copies = [pltpu.make_async_copy(grads_in, grads_out, sems.at[0])]
-    size = lower_in.shape[1] // 4
+def deliver(lower_in, grads_in, lower_out, grads_out, lower_held, grads_held, sems):
+    pieces = [(grads_in, grads_held, grads_out)]
+    size = lower_in.shape[1] // 2
     for i in range(lower_in.shape[0]):
-        for j in range(4):
-            where = pl.ds(size * j, size)
-            copies.append(pltpu.make_async_copy(
-                lower_in.at[i, where], lower_out.at[i, where], sems.at[1 + 4 * i + j]))
-    for copy in copies:
+        for j in range(2):
+            where = (i, pl.ds(size * j, size))
+            pieces.append((lower_in.at[where], lower_held.at[where], lower_out.at[where]))
+    ins = [pltpu.make_async_copy(p[0], p[1], sems.at[0, n]) for n, p in enumerate(pieces)]
+    outs = [pltpu.make_async_copy(p[1], p[2], sems.at[1, n]) for n, p in enumerate(pieces)]
+    for copy in ins:
         copy.start()
-    for copy in copies:
+    for arrived, copy in zip(ins, outs):
+        arrived.wait()
+        copy.start()
+    for copy in outs:
         copy.wait()
 
 
@@ -420,6 +468,7 @@
             pltpu.VMEM((layers, size, chans), bf16),
             pltpu.VMEM((layers, size, chans), bf16),
             pltpu.VMEM((layers, 9, chans, chans), bf16),
+            pltpu.VMEM((layers, 3, 3 * chans, chans), bf16),
             pltpu.VMEM((size, chans), f32),
             pltpu.VMEM((size, chans), f32),
             pltpu.VMEM((size, chans), f32),
@@ -429,7 +478,7 @@
             pltpu.VMEM((size, 3 * chans), bf16),
             pltpu.VMEM((size, 3 * chans), bf16),
             pltpu.VMEM((size, 3 * chans), bf16),
-            pltpu.VMEM((layers * 9, ring, 2, 2, share, chans), f32),
+            pltpu.VMEM((2, layers * 9, ring, 2, share, chans), f32),
             pltpu.VMEM((layers * 9, ring, 2, share, chans), f32),
             pltpu.VMEM((2, ring // 2, layers * 9, 2, share, chans), f32),
             pltpu.VMEM((layers * 9, share, chans), f32),
@@ -443,6 +492,7 @@
             pltpu.SemaphoreType.DMA((2, ring // 2, layers * 9 // PART)),
             pltpu.SemaphoreType.DMA((2, ring // 2, layers * 9 // PART)),
             pltpu.SemaphoreType.DMA((2, layers * 9 // PART)),
+            pltpu.SemaphoreType.DMA((2, len(CROSS_FIRST), ring)),
         ],
         compiler_params=pltpu.CompilerParams(
             collective_id=0, has_side_effects=True, vmem_limit_bytes=60 * 1024 * 1024
@@ -456,7 +506,11 @@
         ),
         in_specs=[any_space] * 2,
         out_specs=(any_space, any_space),
-        scratch_shapes=[pltpu.SemaphoreType.DMA((1 + 4 * images,))],
+        scratch_shapes=[
+            pltpu.VMEM(lower.shape, f32),
+            pltpu.VMEM(grads.shape, f32),
+            pltpu.SemaphoreType.DMA((2, 1 + 2 * images)),
+        ],
     )(lower, grads)
     return (
         lower.reshape(1, images, height, width, chans),

time: 192 us -> 122 us (0.64)
  Pallas kernels: 191 us -> 121 us
    pallas_call x1, Pallas kernels: 69.2 us -> 2.52 us  [on_device(): pl.pallas_call(deliver, out_shape=(jax.ShapeDtypeStruct(lower.shape, f32)...]
    pallas_call x1, Pallas kernels: 122 us -> 119 us  [on_device(): pl.pallas_call(functools.partial(chain_kernel, sections, scale, height, w...]
where the time goes in v4:
time: 122 us
  Pallas kernels  121 us (99%)
    pallas_call x1, Pallas kernels, on_device(): pl.pallas_call(functools.partial(chain_kernel, sections, scale, height, w...  119 us
    pallas_call x1, Pallas kernels, on_device(): pl.pallas_call(deliver, out_shape=(jax.ShapeDtypeStruct(lower.shape, f32)...  2.52 us

profile of v4, /device:TPU:1, one launch (start us, length us, event | category | flops | bytes accessed | tf_op | source)
XLA Modules:
  0.0 121.7 jit_solution(7256755255251962969)
XLA Ops:
  0.6 118.5 %shard_map.59 = (f32[2,1024,256]{2,1,0:T(8,128)}, f32[18,8,256]{2,1,0:T(8,128)}) custom-call(bf16[2,2,1024,256]{3,2,1,0:T(8,128)(2,1)} %bitcast.6, bf16[2,2,1024,256]{3,2,1,0:T(8,128)(2,1)} %bitcast.7, bf16[2,9,256,256]{3,2,1,0:T(8,128)(2,1)} %kernels_hbm.1, f32[2,2,1024,256]{3,2,1,0:T(8,128)} %bitcast.5), custom_call_target="tpu_custom_call" | custom-call | tf_op jit(solution)/shard_map/pallas_call | solution.py:459
  119.2 2.5 %shard_map.60 = (f32[2,1024,256]{2,1,0:T(8,128)}, f32[18,8,256]{2,1,0:T(8,128)}) custom-call(f32[2,1024,256]{2,1,0:T(8,128)} %get-tuple-element.6.lower_in, f32[18,8,256]{2,1,0:T(8,128)} %get-tuple-element.7.grads_in), custom_call_target="tpu_custom_call" | custom-call | tf_op jit(solution)/shard_map/pallas_call | solution.py:501

commit v5 on v4

--- a/solution.py
+++ b/solution.py
@@ -425,24 +425,6 @@
         copy.wait()
 
 
-def deliver(lower_in, grads_in, lower_out, grads_out, lower_held, grads_held, sems):
-    pieces = [(grads_in, grads_held, grads_out)]
-    size = lower_in.shape[1] // 2
-    for i in range(lower_in.shape[0]):
-        for j in range(2):
-            where = (i, pl.ds(size * j, size))
-            pieces.append((lower_in.at[where], lower_held.at[where], lower_out.at[where]))
-    ins = [pltpu.make_async_copy(p[0], p[1], sems.at[0, n]) for n, p in enumerate(pieces)]
-    outs = [pltpu.make_async_copy(p[1], p[2], sems.at[1, n]) for n, p in enumerate(pieces)]
-    for copy in ins:
-        copy.start()
-    for arrived, copy in zip(ins, outs):
-        arrived.wait()
-        copy.start()
-    for copy in outs:
-        copy.wait()
-
-
 def on_device(states, slopes, kernels, guess):
     layers, images, height, width, chans = states.shape
     sections = lax.axis_size("layer")
@@ -459,11 +441,11 @@
     lower, grads = pl.pallas_call(
         functools.partial(chain_kernel, sections, scale, height, width, chans),
         out_shape=(
-            jax.ShapeDtypeStruct((images, pix, chans), f32),
-            jax.ShapeDtypeStruct((layers * 9, chans // replicas, chans), f32),
+            pltpu.VMEM((images, pix, chans), f32),
+            pltpu.VMEM((layers * 9, chans // replicas, chans), f32),
         ),
         in_specs=[any_space] * 4,
-        out_specs=(any_space, any_space),
+        out_specs=(pl.BlockSpec(memory_space=pltpu.VMEM),) * 2,
         scratch_shapes=[
             pltpu.VMEM((layers, size, chans), bf16),
             pltpu.VMEM((layers, size, chans), bf16),
@@ -498,20 +480,6 @@
             collective_id=0, has_side_effects=True, vmem_limit_bytes=60 * 1024 * 1024
         ),
     )(flat(states), flat(slopes), kernels, flat(guess))
-    lower, grads = pl.pallas_call(
-        deliver,
-        out_shape=(
-            jax.ShapeDtypeStruct(lower.shape, f32),
-            jax.ShapeDtypeStruct(grads.shape, f32),
-        ),
-        in_specs=[any_space] * 2,
-        out_specs=(any_space, any_space),
-        scratch_shapes=[
-            pltpu.VMEM(lower.shape, f32),
-            pltpu.VMEM(grads.shape, f32),
-            pltpu.SemaphoreType.DMA((2, 1 + 2 * images)),
-        ],
-    )(lower, grads)
     return (
         lower.reshape(1, images, height, width, chans),
         grads.reshape(layers, 9, share, chans),

time: 122 us -> 120 us (0.984)
  Pallas kernels: 121 us -> 118 us
  local copies, waits for them, and re-layouts: 0 us -> 1.98 us
    pallas_call x1 -> x0, Pallas kernels: 2.52 us -> none  [on_device(): pl.pallas_call(deliver, out_shape=(jax.ShapeDtypeStruct(lower.shape, f32)...]
    unnamed x0 -> x2, local copies, waits for them, and re-layouts: none -> 1.98 us
where the time goes in v5:
time: 120 us
  Pallas kernels  118 us (98%)
  local copies, waits for them, and re-layouts  1.98 us (2%)
    pallas_call x1, Pallas kernels, on_device(): pl.pallas_call(functools.partial(chain_kernel, sections, scale, height, w...  118 us

profile of v5, /device:TPU:1, one launch (start us, length us, event | category | flops | bytes accessed | tf_op | source)
XLA Modules:
  0.0 120.3 jit_solution(7316226800732369542)
XLA Ops:
  0.6 117.7 %shard_map.59 = (f32[2,1024,256]{2,1,0:T(8,128)S(1)}, f32[18,8,256]{2,1,0:T(8,128)S(1)}) custom-call(bf16[2,2,1024,256]{3,2,1,0:T(8,128)(2,1)} %bitcast.8, bf16[2,2,1024,256]{3,2,1,0:T(8,128)(2,1)} %bitcast.9, bf16[2,9,256,256]{3,2,1,0:T(8,128)(2,1)} %kernels_hbm.1, f32[2,2,1024,256]{3,2,1,0:T(8,128)} %bitcast.7), custom_call_target="tpu_custom_call" | custom-call | tf_op jit(solution)/shard_map/pallas_call | solution.py:441
  118.3 1.3 %copy.8 = f32[1,2,32,32,256]{4,3,2,1,0:T(8,128)} copy(f32[1,2,32,32,256]{4,3,2,1,0:T(8,128)S(1)} %bitcast.5) | data formatting | bytes 4194304
  119.6 0.7 copy.9

commit v6 on v5

--- a/solution.py
+++ b/solution.py
@@ -52,10 +52,13 @@
             part = ref.at[rows(start, count)]
             part[...] = jnp.zeros(part.shape, part.dtype)
 
-    first = [load(kernels_hbm.at[0], kern.at[0], load_sems.at[0])]
-    for i in range(2):
-        first.append(load(guess_hbm.at[0, i], image(ends, i), load_sems.at[1 + i]))
-        first.append(load(slopes_hbm.at[0, i], image(slopes.at[0], i), load_sems.at[3 + i]))
+    def load_bottom(i):
+        return [
+            load(guess_hbm.at[0, i], image(ends, i), load_sems.at[1 + i]),
+            load(slopes_hbm.at[0, i], image(slopes.at[0], i), load_sems.at[3 + i]),
+        ]
+
+    first = [load(kernels_hbm.at[0], kern.at[0], load_sems.at[0])] + load_bottom(0)
     place = lax.axis_index("dp")
     ring = lax.axis_size("dp") // 4
     depth = place // 4
@@ -80,19 +83,24 @@
         pl.semaphore_signal(barrier, inc=1, device_id={"layer": s + 1}, device_id_type=MESH)
 
     clear(ends)
-    clear(last)
     clear(slopes.at[0])
-    clear(slopes.at[1])
-    clear(states.at[0])
-    clear(states.at[1])
-    for ref in (z_chain, z_up, z_dn):
-        clear(ref)
-    z_up[rows(-TOP, TOP + 4)] = jnp.zeros(((TOP + 4) * width, 3 * chans), jnp.bfloat16)
-    z_dn[rows(-TOP, TOP + 4)] = jnp.zeros(((TOP + 4) * width, 3 * chans), jnp.bfloat16)
-    grad[...] = jnp.zeros(grad.shape, jnp.float32)
-
-    for copy in first[:3]:
+    clear(z_chain)
+
+    def clear_rest():
+        for ref in (last, slopes.at[1], states.at[0], states.at[1], z_up, z_dn):
+            clear(ref)
+        top = rows(-TOP, TOP + 4)
+        z_up[top] = jnp.zeros(((TOP + 4) * width, 3 * chans), jnp.bfloat16)
+        z_dn[top] = jnp.zeros(((TOP + 4) * width, 3 * chans), jnp.bfloat16)
+        grad[...] = jnp.zeros(grad.shape, jnp.float32)
+
+    @pl.when(h > 0)
+    def _():
+        clear_rest()
+
+    for copy in first:
         copy.wait()
+    second = load_bottom(1)
     rest = [load(kernels_hbm.at[1], kern.at[1], load_sems.at[5])]
     for i in range(2):
         rest.append(load(guess_hbm.at[1, i], image(last, i), load_sems.at[6 + i]))
@@ -116,6 +124,18 @@
             term = jnp.dot(z[rows(start + 1 - a, count), :], kern_t[layer, a],
                            preferred_element_type=jnp.float32)
             total = term if total is None else total + term
+        return total
+
+    def conv_unturned(z, start, count):
+        total = None
+        for a in range(3):
+            for b in range(3):
+                term = lax.dot_general(
+                    z[rows(start + 1 - a, count), b * chans:(b + 1) * chans],
+                    kern[0, 3 * a + b], (((1,), (1,)), ((), ())),
+                    preferred_element_type=jnp.float32,
+                )
+                total = term if total is None else total + term
         return total
 
     def turn(layer):
@@ -172,14 +192,13 @@
 
     blocks = -(-(end_row + 1) // BLK)
     coarse = (end_row - 1) // BLK
-    turn(0)
     spread_end(0)
 
     @pl.loop(0, blocks)
     def _(j):
         @pl.when(j == image_row[1] // BLK - 1)
         def _():
-            for copy in first[3:]:
+            for copy in second:
                 copy.wait()
 
         @pl.when(j < blocks - 1)
@@ -187,7 +206,7 @@
             spread_end(j + 1)
 
         at = rows(BLK * j, BLK)
-        ends[at] = ends[at] + STEP * conv(z_chain, 0, BLK * j, BLK)
+        ends[at] = ends[at] + STEP * conv_unturned(z_chain, BLK * j, BLK)
 
         @pl.when(j == 0)
         def _():
@@ -207,9 +226,13 @@
     def _():
         start_chunk(ends, Q * coarse, BLK * coarse, 1)
 
+    @pl.when(h == 0)
+    def _():
+        clear_rest()
+
+    turn(0)
     for copy in rest:
         copy.wait()
-    turn(1)
 
     @pl.when(h == 0)
     def _():
@@ -274,6 +297,10 @@
             @pl.when(j > 0)
             def _():
                 fine(j, q)
+
+        @pl.when(j == 0)
+        def _():
+            turn(1)
 
     for i in range(BLK):
         step(Q * coarse + i, BLK * coarse + i, 1)

time: 120 us -> 120 us (level)
  no operation moved by 1% of the time
where the time goes in v6:
time: 120 us
  Pallas kernels  117 us (98%)
  local copies, waits for them, and re-layouts  1.98 us (2%)
    pallas_call x1, Pallas kernels, on_device(): pl.pallas_call(functools.partial(chain_kernel, sections, scale, height, w...  117 us

profile of v6, /device:TPU:1, one launch (start us, length us, event | category | flops | bytes accessed | tf_op | source)
XLA Modules:
  0.0 119.8 jit_solution(15971437088848475250)
XLA Ops:
  0.6 117.2 %shard_map.59 = (f32[2,1024,256]{2,1,0:T(8,128)S(1)}, f32[18,8,256]{2,1,0:T(8,128)S(1)}) custom-call(bf16[2,2,1024,256]{3,2,1,0:T(8,128)(2,1)} %bitcast.8, bf16[2,2,1024,256]{3,2,1,0:T(8,128)(2,1)} %bitcast.9, bf16[2,9,256,256]{3,2,1,0:T(8,128)(2,1)} %kernels_hbm.1, f32[2,2,1024,256]{3,2,1,0:T(8,128)} %bitcast.7), custom_call_target="tpu_custom_call" | custom-call | tf_op jit(solution)/shard_map/pallas_call | solution.py:468
  117.8 1.3 %copy.8 = f32[1,2,32,32,256]{4,3,2,1,0:T(8,128)} copy(f32[1,2,32,32,256]{4,3,2,1,0:T(8,128)S(1)} %bitcast.5) | data formatting | bytes 4194304
  119.1 0.7 copy.9
